TPU v7x, 32 devices: a whole 2x2x4 slice. The times are simulated.
32 devices in a mesh: tm: 8 (over y, x, core), strip: 4 (over z).
Axes of the slice: x: 2, y: 2, z: 4, core: 2. Of those that a mesh axis runs over, the one named last changes fastest.
Arguments:
- signal: bfloat16 [2, 16, 16384], P(None, 'strip', 'tm'), may hold values from -5 to 5
Outputs:
- spectrum: bfloat16 [2, 256, 16, 8, 2048], P(None, 'strip', None, 'tm')
All inputs are finite; a program needn't handle non-finite values.
Results may differ from a plain program's by a relative error of at most 0.0069.
Values may be sent and summed in bfloat16 or wider, within the bound.
A program may use at most 128 MiB of HBM per device.

v0:
```python
import math
import jax
import jax.numpy as jnp
from jax import lax
from jax.sharding import PartitionSpec as P

K = 256
TWO_PI = 2.0 * math.pi


def passed_along(value, axis, steps):
    count = lax.axis_size(axis)
    leading, last = (max(0, -steps), min(count, count - steps))
    return lax.ppermute(value, axis, [(source, source + steps) for source in range(leading, last)])


def channel_filters(channel_ids, length):
    offsets = jnp.arange(length, dtype=jnp.int32)
    phases = channel_ids[:, None] * offsets[None, :] % length
    angles = jnp.float32(TWO_PI) * phases.astype(jnp.float32) / length
    hamming = 0.54 - 0.46 * jnp.cos(jnp.float32(TWO_PI) * offsets.astype(jnp.float32) / length)
    scaled = hamming[None, :] / math.sqrt(length)
    cosine = scaled * jnp.cos(angles)
    sine = scaled * jnp.sin(angles)
    real_rows = jnp.stack([cosine, sine], axis=1)
    imag_rows = jnp.stack([-sine, cosine], axis=1)
    return jnp.concatenate([real_rows, imag_rows], axis=0).astype(jnp.bfloat16)


def dft_pair(first, second, modulus, norm):
    phases = first[:, None] * second[None, :] % modulus
    angles = jnp.float32(TWO_PI) * phases.astype(jnp.float32) / modulus
    return (jnp.cos(angles) * norm, jnp.sin(angles) * norm)


def channelize(extended, filters, channel_count, length):
    outcome = lax.conv_general_dilated(
        extended,
        filters,
        (1,),
        "VALID",
        dimension_numbers=("CNH", "OIH", "CNH"),
        preferred_element_type=jnp.float32,
    )
    window_count = extended.shape[1]
    spectra = outcome[:, :, :length].reshape(2, channel_count, window_count, length)
    centered = extended[:, :, K // 2 : K // 2 + length].astype(jnp.float32)
    real_part = spectra[0] * centered[0][None] + spectra[1] * centered[1][None]
    imag_part = spectra[1] * centered[0][None] - spectra[0] * centered[1][None]
    return jnp.stack([real_part, imag_part]).astype(jnp.bfloat16)


def first_pass(values):
    residues = lax.axis_size("tm")
    block_len = values.shape[2]
    piece_len = block_len // residues
    total_len = block_len * residues
    grouped = values.reshape(2, values.shape[1], residues, piece_len)
    res_ids = jnp.arange(residues, dtype=jnp.int32)
    small_cos, small_sin = dft_pair(res_ids, res_ids, residues, 1.0 / math.sqrt(residues))
    small_cos = small_cos.astype(jnp.bfloat16)
    small_sin = small_sin.astype(jnp.bfloat16)
    section_real = jnp.einsum(
        "qn,rns->rqs", small_cos, grouped[0], preferred_element_type=jnp.float32
    ) + jnp.einsum("qn,rns->rqs", small_sin, grouped[1], preferred_element_type=jnp.float32)
    section_imag = jnp.einsum(
        "qn,rns->rqs", small_cos, grouped[1], preferred_element_type=jnp.float32
    ) - jnp.einsum("qn,rns->rqs", small_sin, grouped[0], preferred_element_type=jnp.float32)
    sample_ids = lax.axis_index("tm") * piece_len + jnp.arange(piece_len, dtype=jnp.int32)
    twid_cos, twid_sin = dft_pair(res_ids, sample_ids, total_len, 1.0)
    turned_real = section_real * twid_cos[None] + section_imag * twid_sin[None]
    turned_imag = section_imag * twid_cos[None] - section_real * twid_sin[None]
    turned = jnp.stack([turned_real, turned_imag]).astype(jnp.bfloat16)
    return turned.reshape(2, values.shape[1], residues * piece_len)


def second_pass(values):
    block_len = values.shape[2]
    blk_ids = jnp.arange(block_len, dtype=jnp.int32)
    big_cos, big_sin = dft_pair(blk_ids, blk_ids, block_len, 1.0 / math.sqrt(block_len))
    big_cos = big_cos.astype(jnp.bfloat16)
    big_sin = big_sin.astype(jnp.bfloat16)
    out_real = jnp.dot(values[0], big_cos, preferred_element_type=jnp.float32) + jnp.dot(
        values[1], big_sin, preferred_element_type=jnp.float32
    )
    out_imag = jnp.dot(values[1], big_cos, preferred_element_type=jnp.float32) - jnp.dot(
        values[0], big_sin, preferred_element_type=jnp.float32
    )
    return jnp.stack([out_real, out_imag]).astype(jnp.bfloat16)


def per_device(signal):
    block_len = signal.shape[2]
    local_chan = K // lax.axis_size("strip")
    following = passed_along(signal[:, :, :K], "tm", -1)
    extended = jnp.concatenate([signal, following], axis=2)
    every_window = lax.all_gather(extended, "strip", axis=1, tiled=True)
    channel_ids = lax.axis_index("strip") * local_chan + jnp.arange(local_chan, dtype=jnp.int32)
    filters = channel_filters(channel_ids, K)
    products = channelize(every_window, filters, local_chan, block_len)
    window_total = products.shape[2]
    strips = products.reshape(2, local_chan * window_total, block_len)
    partial_sums = first_pass(lax.all_to_all(strips, "tm", split_axis=2, concat_axis=2, tiled=True))
    finished = second_pass(
        lax.all_to_all(partial_sums, "tm", split_axis=2, concat_axis=2, tiled=True)
    )
    return finished.reshape(2, local_chan, window_total, 1, block_len)


def solution(mesh):
    placed = (P(None, "strip", "tm"),)
    return jax.shard_map(
        per_device,
        mesh=mesh,
        in_specs=placed,
        out_specs=P(None, "strip", None, "tm", None),
        check_vma=False,
    )
```

profile of v0, /device:TPU:0, one launch (start us, length us, event | category | flops | bytes accessed | tf_op | source)
XLA Modules:
  0.0 851.7 jit_solution(14918469817403316897)
XLA Ops:
  0.0 0.7 slice.45
  0.7 1.3 collective-permute-start
  2.0 0.3 fusion.28
  2.4 0.1 copy.42
  2.5 1.2 collective-permute-done
  3.7 0.8 pad_maximum_fusion.3
  4.6 15.4 %all_gather.3 = bf16[2,16,2304]{2,0,1:T(2,128)(2,1)S(1)} all-gather(bf16[2,4,2304]{2,0,1:T(2,128)(2,1)S(1)} %copy.40), channel_id=1, replica_groups=mesh['tm'=8,'strip'=4] {'strip'}, dimensions={1}, use_global_device_ids=true | all-gather | bytes 184320 | tf_op jit(solution)/shard_map/all_gather | solution.py:97
  20.0 1.6 copy.41
  21.6 0.1 slice_convert_fusion
  21.7 0.2 fusion.95
  22.0 1.3 copy.56
  23.3 1.3 copy.57
  24.6 0.0 copy-start.3
  24.6 135.8 %fusion.96 = f32[128,16,2048]{0,1,2:T(8,128)S(1)} fusion(bf16[2,16,2304]{1,0,2:T(2,128)(2,1)S(1)} %copy.41, bf16[128,2,256]{0,1,2:T(2,128)(2,1)S(1)} %copy.42), kind=kOutput, calls=%fused_computation.124 | convolution fusion | flops 4294967296 | bytes 17055744 | tf_op jit(solution)/shard_map/slice | solution.py:46
  160.4 0.0 copy-done.3
  160.4 0.0 copy-done.4
  160.4 16.4 %add_convert_fusion = (bf16[64,16,2048]{0,1,2:T(8,128)(2,1)}, bf16[64,16,2048]{0,1,2:T(8,128)(2,1)}) fusion(f32[128,16,2048]{0,1,2:T(8,128)S(1)} %fusion.96, f32[16,2048]{0,1:T(8,128)S(1)} %bitcast.78, f32[16,2048]{0,1:T(8,128)S(1)} %bitcast.77), kind=kLoop, calls=%fused_computation.11 | loop fusion | flops 16777216 | bytes 25427968 | tf_op jit(solution)/shard_map/convert.11
  176.8 12.0 %copy.45 = bf16[64,16,2048]{2,1,0:T(8,128)(2,1)} copy(bf16[64,16,2048]{0,1,2:T(8,128)(2,1)} %get-tuple-element.7) | data formatting | bytes 8388608 | tf_op jit(solution)/shard_map/convert.11
  188.8 12.1 %copy.46 = bf16[64,16,2048]{2,1,0:T(8,128)(2,1)} copy(bf16[64,16,2048]{0,1,2:T(8,128)(2,1)} %get-tuple-element.8) | data formatting | bytes 8388608 | tf_op jit(solution)/shard_map/convert.10
  200.9 7.6 pad_maximum_fusion
  208.5 21.4 %copy.47 = bf16[2,1024,2048]{1,0,2:T(2,128)(2,1)} copy(bf16[2,1024,2048]{2,1,0:T(8,128)(2,1)} %pad_maximum_fusion) | data formatting | bytes 16777216 | tf_op jit(solution)/shard_map/stack | solution.py:50
  229.9 5.1 all-to-all-start
  235.1 0.1 fusion.39
  235.2 94.0 %all-to-all-done = bf16[2,1024,2048]{1,0,2:T(2,128)(2,1)} async-done(((bf16[2,1024,2048]{1,0,2:T(2,128)(2,1)}), bf16[2,1024,2048]{1,0,2:T(2,128)(2,1)}, u32[]{:S(2)}, u32[]{:S(2)}) %all-to-all-start) | async-done | bytes 8388640 | tf_op jit(solution)/shard_map/all_to_all | solution.py:103
  329.1 17.4 %fusion.94 = (bf16[1,1024,2048]{1,0,2:T(2,128)(2,1)S(1)}, bf16[1,1024,2048]{1,0,2:T(2,128)(2,1)}) fusion(bf16[2,1024,2048]{1,0,2:T(2,128)(2,1)} %all-to-all-done), kind=kLoop, calls=%fused_computation.122 | loop fusion | bytes 16777216 | tf_op jit(solution)/shard_map/slice | solution.py:64
  346.5 3.7 copy.60
  350.3 6.9 copy.58
  357.2 0.0 copy-start
  357.2 6.9 fusion.45
  364.1 0.0 copy-done
  364.1 4.5 fusion.51
  368.6 0.0 slice-done
  368.6 0.0 slice-done.1
  368.6 3.7 copy.61
  372.3 7.2 copy.59
  379.5 6.9 fusion.47
  386.4 15.8 %fusion.7 = (bf16[1024,8,256]{2,1,0:T(8,128)(2,1)}, bf16[1024,8,256]{2,1,0:T(8,128)(2,1)}) fusion(f32[8,256]{1,0:T(8,128)S(1)} %get-tuple-element.19, f32[8,256]{1,0:T(8,128)S(1)} %get-tuple-element.18, f32[1024,256,8]{1,2,0:T(8,128)} %fusion.45, f32[1024,256,8]{1,2,0:T(8,128)} %fusion.51, f32[1024,256,8]{1,2,0:T(8,128)} %fusion.47, ...), kind=kOutput, calls=%fused_computation.19 | convolution fusion | flops 54526976 | bytes 37765120 | tf_op jit(solution)/shard_map/qn,rns->rqs/dot_general | solution.py:66
  402.1 7.4 stack.44
  409.5 20.6 %copy.50 = bf16[1,1024,2048]{1,0,2:T(2,128)(2,1)} copy(bf16[1,1024,2048]{2,1,0:T(8,128)(2,1)} %stack.44) | data formatting | bytes 8388608 | tf_op jit(solution)/shard_map/stack | solution.py:73
  430.0 7.4 stack.45
  437.4 20.3 %copy.51 = bf16[1,1024,2048]{1,0,2:T(2,128)(2,1)} copy(bf16[1,1024,2048]{2,1,0:T(8,128)(2,1)} %stack.45) | data formatting | bytes 8388608 | tf_op jit(solution)/shard_map/stack | solution.py:73
  457.7 19.7 %pad_maximum_fusion.1 = bf16[2,1024,2048]{1,0,2:T(2,128)(2,1)} fusion(bf16[1,1024,2048]{1,0,2:T(2,128)(2,1)} %copy.51, bf16[1,1024,2048]{1,0,2:T(2,128)(2,1)} %copy.50), kind=kLoop, calls=%fused_computation.14 | loop fusion | flops 16777216 | bytes 16777216 | tf_op jit(solution)/shard_map/stack | solution.py:73
  477.4 5.2 all-to-all-start.1
  482.6 62.8 %multiply_convert_fusion.22 = bf16[2048,2048]{1,0:T(8,128)(2,1)} fusion(), kind=kLoop, calls=%fused_computation.7.clone.1.clone | loop fusion | flops 67108864 | bytes 8388608 | tf_op jit(solution)/shard_map/dot_general | solution.py:83
  545.4 63.3 %multiply_convert_fusion.20 = bf16[2048,2048]{1,0:T(8,128)(2,1)} fusion(), kind=kLoop, calls=%fused_computation.6.clone.1.clone.clone.clone.1 | loop fusion | flops 67108864 | bytes 8388608 | tf_op jit(solution)/shard_map/dot_general | solution.py:83
  608.7 62.8 %multiply_convert_fusion.21 = bf16[2048,2048]{1,0:T(8,128)(2,1)} fusion(), kind=kLoop, calls=%fused_computation.7.clone.clone.1 | loop fusion | flops 67108864 | bytes 8388608 | tf_op jit(solution)/shard_map/dot_general | solution.py:86
  671.5 63.3 %multiply_convert_fusion.19 = bf16[2048,2048]{1,0:T(8,128)(2,1)} fusion(), kind=kLoop, calls=%fused_computation.6.clone.clone.clone.clone.1 | loop fusion | flops 67108864 | bytes 8388608 | tf_op jit(solution)/shard_map/dot_general | solution.py:86
  734.8 0.0 all-to-all-done.1
  734.8 17.6 %fusion.93 = (bf16[1,1024,2048]{1,0,2:T(2,128)(2,1)}, bf16[1,1024,2048]{1,0,2:T(2,128)(2,1)}) fusion(bf16[2,1024,2048]{1,0,2:T(2,128)(2,1)} %all-to-all-done.1), kind=kLoop, calls=%fused_computation.121 | loop fusion | bytes 16777216 | tf_op jit(solution)/shard_map/slice | solution.py:83
  752.4 20.1 %copy.62 = bf16[1,1024,2048]{2,1,0:T(8,128)(2,1)} copy(bf16[1,1024,2048]{1,0,2:T(2,128)(2,1)} %get-tuple-element.9) | data formatting | bytes 8388608
  772.5 19.8 %copy.63 = bf16[1,1024,2048]{2,1,0:T(8,128)(2,1)} copy(bf16[1,1024,2048]{1,0,2:T(2,128)(2,1)} %get-tuple-element.10) | data formatting | bytes 8388608
  792.3 14.9 %fusion.11 = f32[1024,2048]{1,0:T(8,128)} fusion(bf16[1,1024,2048]{2,1,0:T(8,128)(2,1)} %copy.62, bf16[2048,2048]{1,0:T(8,128)(2,1)} %multiply_convert_fusion.22), kind=kOutput, calls=%fused_computation.27 | convolution fusion | flops 8589934592 | bytes 20971520 | tf_op jit(solution)/shard_map/dot_general | solution.py:83
  807.2 0.0 copy-done.2
  807.2 13.3 %fusion.10 = f32[1024,2048]{1,0:T(8,128)} fusion(bf16[1,1024,2048]{2,1,0:T(8,128)(2,1)S(1)} %copy-done.2, bf16[2048,2048]{1,0:T(8,128)(2,1)} %multiply_convert_fusion.21), kind=kOutput, calls=%fused_computation.26 | convolution fusion | flops 8589934592 | bytes 20971520 | tf_op jit(solution)/shard_map/dot_general | solution.py:86
  820.5 0.0 slice-done.4
  820.5 0.0 slice-done.5
  820.5 12.1 %add_convert_fusion.1 = bf16[1024,2048]{1,0:T(8,128)(2,1)} fusion(f32[1024,2048]{1,0:T(8,128)} %fusion.11, bf16[1,1024,2048]{2,1,0:T(8,128)(2,1)S(1)} %copy-done.2, bf16[2048,2048]{1,0:T(8,128)(2,1)S(1)} %bitcast.76), kind=kOutput, calls=%fused_computation.25 | convolution fusion | flops 8594128896 | bytes 25165824 | tf_op jit(solution)/shard_map/dot_general | solution.py:83
  832.7 0.0 slice-done.2
  832.7 0.0 slice-done.3
  832.7 0.0 copy-done.1
  832.7 0.0 copy-start.5
  832.7 12.1 %subtract_convert_fusion.1 = bf16[1024,2048]{1,0:T(8,128)(2,1)} fusion(f32[1024,2048]{1,0:T(8,128)} %fusion.10, bf16[1,1024,2048]{2,1,0:T(8,128)(2,1)S(1)} %copy-done.1, bf16[2048,2048]{1,0:T(8,128)(2,1)S(1)} %bitcast.74), kind=kOutput, calls=%fused_computation.24 | convolution fusion | flops 8594128896 | bytes 25165824 | tf_op jit(solution)/shard_map/dot_general | solution.py:86
  844.9 0.0 copy-done.5
  844.9 6.3 pad_maximum_fusion.2
  (17 shorter events, 0.1 us)
Async XLA Ops:
  0.7 3.0 collective-permute-start
  24.6 135.8 %copy-start.3 = (f32[1,16,2048]{1,2,0:T(8,128)S(1)}, f32[1,16,2048]{1,2,0:T(8,128)}, u32[]{:S(2)}) copy-start(f32[1,16,2048]{1,2,0:T(8,128)} %copy.56) | copy-start | bytes 393220
  24.6 135.8 %copy-start.4 = (f32[1,16,2048]{1,2,0:T(8,128)S(1)}, f32[1,16,2048]{1,2,0:T(8,128)}, u32[]{:S(2)}) copy-start(f32[1,16,2048]{1,2,0:T(8,128)} %copy.57) | copy-start | bytes 393220
  229.9 99.2 %all-to-all-start = ((bf16[2,1024,2048]{1,0,2:T(2,128)(2,1)}), bf16[2,1024,2048]{1,0,2:T(2,128)(2,1)}, u32[]{:S(2)}, u32[]{:S(2)}) async-start(bf16[2,1024,2048]{1,0,2:T(2,128)(2,1)} %copy.47), calls=%async_computation | async-start | bytes 16777216 | tf_op jit(solution)/shard_map/all_to_all | solution.py:103
  357.2 6.9 copy-start
  357.2 11.4 %slice-start = ((s8[8388608]{0:T(1024)(128)(4,1)}), s8[4194304]{0:T(1024)(128)(4,1)S(1)}, s32[]{:S(2)}) async-start(s8[8388608]{0:T(1024)(128)(4,1)} %bitcast.67), calls=%async_computation.2 | async-start | bytes 8388608
  364.1 4.5 slice-start.1
  477.4 257.4 %all-to-all-start.1 = ((bf16[2,1024,2048]{1,0,2:T(2,128)(2,1)}), bf16[2,1024,2048]{1,0,2:T(2,128)(2,1)}, u32[]{:S(2)}, u32[]{:S(2)}) async-start(bf16[2,1024,2048]{1,0,2:T(2,128)(2,1)} %pad_maximum_fusion.1), calls=%async_computation.1 | async-start | bytes 16777216 | tf_op jit(solution)/shard_map/all_to_all | solution.py:105
  792.3 14.9 %copy-start.2 = (bf16[1,1024,2048]{2,1,0:T(8,128)(2,1)S(1)}, bf16[1,1024,2048]{2,1,0:T(8,128)(2,1)}, u32[]{:S(2)}) copy-start(bf16[1,1024,2048]{2,1,0:T(8,128)(2,1)} %copy.63) | copy-start | bytes 12582916
  792.3 28.2 %slice-start.4 = ((s8[8388608]{0:T(1024)(128)(4,1)}), s8[4194304]{0:T(1024)(128)(4,1)S(1)}, s32[]{:S(2)}) async-start(s8[8388608]{0:T(1024)(128)(4,1)} %bitcast.75), calls=%async_computation.6 | async-start | bytes 8388608
  792.3 40.4 %slice-start.2 = ((s8[8388608]{0:T(1024)(128)(4,1)}), s8[4194304]{0:T(1024)(128)(4,1)S(1)}, s32[]{:S(2)}) async-start(s8[8388608]{0:T(1024)(128)(4,1)} %bitcast.73), calls=%async_computation.4 | async-start | bytes 8388608
  807.2 13.4 %slice-start.5 = ((s8[8388608]{0:T(1024)(128)(4,1)}), s8[4194304]{0:T(1024)(128)(4,1)S(1)}, s32[]{:S(2)}) async-start(s8[8388608]{0:T(1024)(128)(4,1)} %bitcast.75), calls=%async_computation.7 | async-start | bytes 8388608
  807.2 25.5 %slice-start.3 = ((s8[8388608]{0:T(1024)(128)(4,1)}), s8[4194304]{0:T(1024)(128)(4,1)S(1)}, s32[]{:S(2)}) async-start(s8[8388608]{0:T(1024)(128)(4,1)} %bitcast.73), calls=%async_computation.5 | async-start | bytes 8388608
  820.5 12.2 %copy-start.1 = (bf16[1,1024,2048]{2,1,0:T(8,128)(2,1)S(1)}, bf16[1,1024,2048]{2,1,0:T(8,128)(2,1)}, u32[]{:S(2)}) copy-start(bf16[1,1024,2048]{2,1,0:T(8,128)(2,1)} %copy.62) | copy-start | bytes 12582916
  832.7 12.1 %copy-start.5 = (bf16[1024,2048]{1,0:T(8,128)(2,1)S(1)}, bf16[1024,2048]{1,0:T(8,128)(2,1)}, u32[]{:S(2)}) copy-start(bf16[1024,2048]{1,0:T(8,128)(2,1)} %add_convert_fusion.1) | copy-start | bytes 12582916
where the time goes:
time: 858 us; the launch traced here: 852 us
  other arithmetic  304 us (35%)
  matrix products  222 us (26%)
  local copies, waits for them, and re-layouts  203 us (24%)
  waiting for transfers between devices  95.2 us (11%)
  blocking collectives  15.4 us (2%)
  starting transfers between devices  11.6 us (1%)
    slice x1, matrix products, channelize(): outcome[:, :, :length].reshape(2, channel_count, window_count, length)  136 us
    all_to_all x1, waiting for transfers between devices, per_device(): lax.all_to_all(strips, 'tm', split_axis=2, concat_axis=2, tiled=True)  94 us
    dot_general x1, other arithmetic, second_pass(): jnp.dot(values[0], big_sin, preferred_element_type=jnp.float32)  63.3 us
    dot_general x1, other arithmetic, second_pass(): jnp.dot(values[1], big_sin, preferred_element_type=jnp.float32)  63.3 us
    dot_general x1, other arithmetic, second_pass(): jnp.dot(values[0], big_cos, preferred_element_type=jnp.float32)  62.8 us
    dot_general x1, other arithmetic, second_pass(): jnp.dot(values[1], big_cos, preferred_element_type=jnp.float32)  62.8 us
    another operation x4, local copies, waits for them, and re-layouts, first_pass(): turned = jnp.stack([turned_real, turned_imag]).astype(jnp.bfloat16)  55.5 us
    unnamed x28, local copies, waits for them, and re-layouts  47.4 us
  transfers between devices with their start and end apart: 3, of which 2 were waited for; matrix products, arithmetic and copies ran while one was open for 30% of the time, Pallas kernels for 0%

commit v1 on v0

--- a/solution.py
+++ b/solution.py
@@ -100,7 +100,12 @@
     products = channelize(every_window, filters, local_chan, block_len)
     window_total = products.shape[2]
     strips = products.reshape(2, local_chan * window_total, block_len)
-    partial_sums = first_pass(lax.all_to_all(strips, "tm", split_axis=2, concat_axis=2, tiled=True))
+    partial_sums = first_pass(
+        jnp.concatenate(
+            lax.all_to_all(jnp.stack(jnp.split(strips, lax.axis_size("tm"), axis=2)), "tm", 0, 0),
+            axis=2,
+        )
+    )
     finished = second_pass(
         lax.all_to_all(partial_sums, "tm", split_axis=2, concat_axis=2, tiled=True)
     )

time: 858 us -> 817 us (0.952)
  local copies, waits for them, and re-layouts: 203 us -> 156 us
    another operation x3 -> x2, local copies, waits for them, and re-layouts: 45.5 us -> 24 us
    slice x1 -> x0, local copies, waits for them, and re-layouts: 17.4 us -> none  [first_pass(): grouped[0]]
    squeeze x2 -> x0, local copies, waits for them, and re-layouts: 14.1 us -> none  [the longest x1 7.15 us: first_pass(): grouped[1]]
    all_to_all x0 -> x1, local copies, waits for them, and re-layouts: none -> 11.6 us  [per_device(): lax.all_to_all(jnp.stack(jnp.split(strips, lax.axis_size('tm'), axis=2)),...]
    unnamed x3 -> x9, other arithmetic: 0.01 us -> 9.11 us
    unnamed x28 -> x26, local copies, waits for them, and re-layouts: 47.4 us -> 41.8 us
  transfers between devices with their start and end apart: 3 -> 3, of which waited for: 2 -> 2; matrix products, arithmetic and copies ran while one was open for 30% -> 31% of each run, Pallas kernels for 0% -> 0%
where the time goes in v1:
time: 817 us; the launch traced here: 811 us
  other arithmetic  307 us (38%)
  matrix products  227 us (28%)
  local copies, waits for them, and re-layouts  156 us (19%)
  waiting for transfers between devices  95.2 us (12%)
  blocking collectives  15.4 us (2%)
  starting transfers between devices  11.4 us (1%)
    slice x1, matrix products, channelize(): outcome[:, :, :length].reshape(2, channel_count, window_count, length)  144 us
    all_to_all x1, waiting for transfers between devices, per_device(): lax.all_to_all(jnp.stack(jnp.split(strips, lax.axis_size('tm'), axis=2)),...  94 us
    dot_general x1, other arithmetic, second_pass(): jnp.dot(values[0], big_sin, preferred_element_type=jnp.float32)  63.3 us
    dot_general x1, other arithmetic, second_pass(): jnp.dot(values[1], big_sin, preferred_element_type=jnp.float32)  63.3 us
    dot_general x1, other arithmetic, second_pass(): jnp.dot(values[0], big_cos, preferred_element_type=jnp.float32)  62.8 us
    dot_general x1, other arithmetic, second_pass(): jnp.dot(values[1], big_cos, preferred_element_type=jnp.float32)  62.8 us
    another operation x4, local copies, waits for them, and re-layouts, first_pass(): turned = jnp.stack([turned_real, turned_imag]).astype(jnp.bfloat16)  55.6 us
    unnamed x26, local copies, waits for them, and re-layouts  41.8 us
  transfers between devices with their start and end apart: 3, of which 2 were waited for; matrix products, arithmetic and copies ran while one was open for 31% of the time, Pallas kernels for 0%

profile of v1, /device:TPU:0, one launch (start us, length us, event | category | flops | bytes accessed | tf_op | source)
XLA Modules:
  0.0 811.4 jit_solution(144018718931603277)
XLA Ops:
  0.0 0.7 slice.43
  0.7 1.3 collective-permute-start
  2.0 0.3 fusion.41
  2.4 0.1 copy.144
  2.5 1.2 collective-permute-done
  3.7 0.8 pad_maximum_fusion.3
  4.6 15.4 %all_gather.3 = bf16[2,16,2304]{2,0,1:T(2,128)(2,1)S(1)} all-gather(bf16[2,4,2304]{2,0,1:T(2,128)(2,1)S(1)} %copy.142), channel_id=1, replica_groups=mesh['tm'=8,'strip'=4] {'strip'}, dimensions={1}, use_global_device_ids=true | all-gather | bytes 184320 | tf_op jit(solution)/shard_map/all_gather | solution.py:97
  20.0 1.6 copy.143
  21.6 0.1 slice_convert_fusion
  21.7 0.2 fusion.103
  22.0 1.4 copy.156
  23.3 1.3 copy.157
  24.6 144.3 %fusion.104 = f32[128,16,2048]{0,1,2:T(8,128)S(1)} fusion(bf16[2,16,2304]{1,0,2:T(2,128)(2,1)S(1)} %copy.143, bf16[128,2,256]{0,1,2:T(2,128)(2,1)S(1)} %copy.144), kind=kOutput, calls=%fused_computation.156 | convolution fusion | flops 4294967296 | bytes 17055744 | tf_op jit(solution)/shard_map/slice | solution.py:46
  169.0 0.0 copy-done.5
  169.0 0.0 copy-done.6
  169.0 16.4 %add_convert_fusion = (bf16[64,16,2048]{0,1,2:T(8,128)(2,1)}, bf16[64,16,2048]{0,1,2:T(8,128)(2,1)}) fusion(f32[128,16,2048]{0,1,2:T(8,128)S(1)} %fusion.104, f32[16,2048]{0,1:T(8,128)S(1)} %bitcast.117, f32[16,2048]{0,1:T(8,128)S(1)} %bitcast.116), kind=kLoop, calls=%fused_computation.11 | loop fusion | flops 16777216 | bytes 25427968 | tf_op jit(solution)/shard_map/convert.11
  185.4 12.0 %copy.147 = bf16[64,16,2048]{2,1,0:T(8,128)(2,1)} copy(bf16[64,16,2048]{0,1,2:T(8,128)(2,1)} %get-tuple-element.7) | data formatting | bytes 8388608 | tf_op jit(solution)/shard_map/convert.11
  197.4 12.0 %copy.148 = bf16[64,16,2048]{2,1,0:T(8,128)(2,1)} copy(bf16[64,16,2048]{0,1,2:T(8,128)(2,1)} %get-tuple-element.8) | data formatting | bytes 8388608 | tf_op jit(solution)/shard_map/convert.10
  209.4 2.4 bitcast_dynamic-update-slice_fusion.6
  211.8 0.5 copy-done
  212.3 1.3 copy-done.1
  213.6 1.1 bitcast_dynamic-update-slice_fusion.5
  214.7 1.1 bitcast_dynamic-update-slice_fusion.4
  215.8 1.1 bitcast_dynamic-update-slice_fusion.3
  216.9 1.1 bitcast_dynamic-update-slice_fusion.2
  218.0 1.1 bitcast_dynamic-update-slice_fusion.1
  219.2 1.1 bitcast_dynamic-update-slice_fusion
  220.3 1.1 fusion.34
  221.4 5.2 all-to-all-start
  226.6 0.1 fusion.52
  226.6 94.0 %all-to-all-done = bf16[8,2,1024,256]{3,2,1,0:T(8,128)(2,1)} async-done(((bf16[8,2,1024,256]{3,2,1,0:T(8,128)(2,1)}), bf16[8,2,1024,256]{3,2,1,0:T(8,128)(2,1)}, u32[]{:S(2)}, u32[]{:S(2)}) %all-to-all-start) | async-done | bytes 8388640 | tf_op jit(solution)/shard_map/all_to_all | solution.py:105
  320.6 11.6 %copy.161 = bf16[8,2,1024,256]{3,0,2,1:T(8,128)(2,1)} copy(bf16[8,2,1024,256]{3,2,1,0:T(8,128)(2,1)} %all-to-all-done) | data formatting | bytes 16777216 | tf_op jit(solution)/shard_map/all_to_all | solution.py:105
  332.2 6.9 fusion.18
  339.1 0.0 copy-done.2
  339.1 4.7 fusion.19
  343.7 4.5 fusion.21
  348.2 13.6 %fusion.7 = (bf16[1024,8,256]{2,1,0:T(8,128)(2,1)}, bf16[1024,8,256]{2,1,0:T(8,128)(2,1)}) fusion(f32[8,256]{1,0:T(8,128)S(1)} %get-tuple-element.17, f32[8,256]{1,0:T(8,128)S(1)} %get-tuple-element.16, f32[1024,256,8]{1,2,0:T(8,128)} %fusion.18, f32[1024,256,8]{1,2,0:T(8,128)} %fusion.19, f32[1024,256,8]{1,2,0:T(8,128)} %fusion.21, ...), kind=kOutput, calls=%fused_computation.32 | convolution fusion | flops 54526976 | bytes 37765120 | tf_op jit(solution)/shard_map/qn,rns->rqs/dot_general | solution.py:66
  361.9 7.4 stack.80
  369.2 20.6 %copy.150 = bf16[1,1024,2048]{1,0,2:T(2,128)(2,1)} copy(bf16[1,1024,2048]{2,1,0:T(8,128)(2,1)} %stack.80) | data formatting | bytes 8388608 | tf_op jit(solution)/shard_map/stack | solution.py:73
  389.9 7.4 stack.81
  397.2 20.3 %copy.151 = bf16[1,1024,2048]{1,0,2:T(2,128)(2,1)} copy(bf16[1,1024,2048]{2,1,0:T(8,128)(2,1)} %stack.81) | data formatting | bytes 8388608 | tf_op jit(solution)/shard_map/stack | solution.py:73
  417.5 20.0 %pad_maximum_fusion = bf16[2,1024,2048]{1,0,2:T(2,128)(2,1)} fusion(bf16[1,1024,2048]{1,0,2:T(2,128)(2,1)} %copy.151, bf16[1,1024,2048]{1,0,2:T(2,128)(2,1)} %copy.150), kind=kLoop, calls=%fused_computation.27 | loop fusion | flops 16777216 | bytes 16777216 | tf_op jit(solution)/shard_map/stack | solution.py:73
  437.5 5.0 all-to-all-start.1
  442.5 62.8 %multiply_convert_fusion.22 = bf16[2048,2048]{1,0:T(8,128)(2,1)} fusion(), kind=kLoop, calls=%fused_computation.7.clone.1.clone | loop fusion | flops 67108864 | bytes 8388608 | tf_op jit(solution)/shard_map/dot_general | solution.py:83
  505.3 63.3 %multiply_convert_fusion.20 = bf16[2048,2048]{1,0:T(8,128)(2,1)} fusion(), kind=kLoop, calls=%fused_computation.6.clone.1.clone.clone.clone.1 | loop fusion | flops 67108864 | bytes 8388608 | tf_op jit(solution)/shard_map/dot_general | solution.py:83
  568.6 62.8 %multiply_convert_fusion.21 = bf16[2048,2048]{1,0:T(8,128)(2,1)} fusion(), kind=kLoop, calls=%fused_computation.7.clone.clone.1 | loop fusion | flops 67108864 | bytes 8388608 | tf_op jit(solution)/shard_map/dot_general | solution.py:86
  631.4 63.3 %multiply_convert_fusion.19 = bf16[2048,2048]{1,0:T(8,128)(2,1)} fusion(), kind=kLoop, calls=%fused_computation.6.clone.clone.clone.clone.1 | loop fusion | flops 67108864 | bytes 8388608 | tf_op jit(solution)/shard_map/dot_general | solution.py:86
  694.7 0.0 all-to-all-done.1
  694.7 17.5 %fusion.102 = (bf16[1,1024,2048]{1,0,2:T(2,128)(2,1)}, bf16[1,1024,2048]{1,0,2:T(2,128)(2,1)}) fusion(bf16[2,1024,2048]{1,0,2:T(2,128)(2,1)} %all-to-all-done.1), kind=kLoop, calls=%fused_computation.154 | loop fusion | bytes 16777216 | tf_op jit(solution)/shard_map/slice | solution.py:83
  712.2 20.1 %copy.158 = bf16[1,1024,2048]{2,1,0:T(8,128)(2,1)} copy(bf16[1,1024,2048]{1,0,2:T(2,128)(2,1)} %get-tuple-element.9) | data formatting | bytes 8388608
  732.3 19.8 %copy.159 = bf16[1,1024,2048]{2,1,0:T(8,128)(2,1)} copy(bf16[1,1024,2048]{1,0,2:T(2,128)(2,1)} %get-tuple-element.10) | data formatting | bytes 8388608
  752.2 14.9 %fusion.11 = f32[1024,2048]{1,0:T(8,128)} fusion(bf16[1,1024,2048]{2,1,0:T(8,128)(2,1)} %copy.158, bf16[2048,2048]{1,0:T(8,128)(2,1)} %multiply_convert_fusion.22), kind=kOutput, calls=%fused_computation.41 | convolution fusion | flops 8589934592 | bytes 20971520 | tf_op jit(solution)/shard_map/dot_general | solution.py:83
  767.1 0.0 copy-done.4
  767.1 13.3 %fusion.10 = f32[1024,2048]{1,0:T(8,128)} fusion(bf16[1,1024,2048]{2,1,0:T(8,128)(2,1)S(1)} %copy-done.4, bf16[2048,2048]{1,0:T(8,128)(2,1)} %multiply_convert_fusion.21), kind=kOutput, calls=%fused_computation.40 | convolution fusion | flops 8589934592 | bytes 20971520 | tf_op jit(solution)/shard_map/dot_general | solution.py:86
  780.5 0.0 slice-done.2
  780.5 0.0 slice-done.3
  780.5 12.2 %add_convert_fusion.1 = bf16[1024,2048]{1,0:T(8,128)(2,1)} fusion(f32[1024,2048]{1,0:T(8,128)} %fusion.11, bf16[1,1024,2048]{2,1,0:T(8,128)(2,1)S(1)} %copy-done.4, bf16[2048,2048]{1,0:T(8,128)(2,1)S(1)} %bitcast.115), kind=kOutput, calls=%fused_computation.39 | convolution fusion | flops 8594128896 | bytes 25165824 | tf_op jit(solution)/shard_map/dot_general | solution.py:83
  792.6 0.0 slice-done
  792.6 0.0 slice-done.1
  792.6 0.0 copy-done.3
  792.7 0.0 copy-start.7
  792.7 12.1 %subtract_convert_fusion.1 = bf16[1024,2048]{1,0:T(8,128)(2,1)} fusion(f32[1024,2048]{1,0:T(8,128)} %fusion.10, bf16[1,1024,2048]{2,1,0:T(8,128)(2,1)S(1)} %copy-done.3, bf16[2048,2048]{1,0:T(8,128)(2,1)S(1)} %bitcast.113), kind=kOutput, calls=%fused_computation.38 | convolution fusion | flops 8594128896 | bytes 25165824 | tf_op jit(solution)/shard_map/dot_general | solution.py:86
  804.8 0.0 copy-done.7
  804.8 6.3 pad_maximum_fusion.1
  (18 shorter events, 0.1 us)
Async XLA Ops:
  0.7 3.0 collective-permute-start
  24.6 144.3 %copy-start.5 = (f32[1,16,2048]{1,2,0:T(8,128)S(1)}, f32[1,16,2048]{1,2,0:T(8,128)}, u32[]{:S(2)}) copy-start(f32[1,16,2048]{1,2,0:T(8,128)} %copy.156) | copy-start | bytes 393220
  24.6 144.3 %copy-start.6 = (f32[1,16,2048]{1,2,0:T(8,128)S(1)}, f32[1,16,2048]{1,2,0:T(8,128)}, u32[]{:S(2)}) copy-start(f32[1,16,2048]{1,2,0:T(8,128)} %copy.157) | copy-start | bytes 393220
  209.4 2.9 copy-start
  209.4 4.2 copy-start.1
  221.4 99.2 %all-to-all-start = ((bf16[8,2,1024,256]{3,2,1,0:T(8,128)(2,1)}), bf16[8,2,1024,256]{3,2,1,0:T(8,128)(2,1)}, u32[]{:S(2)}, u32[]{:S(2)}) async-start(bf16[8,2,1024,256]{3,2,1,0:T(8,128)(2,1)} %fusion.34), calls=%async_computation | async-start | bytes 16777216 | tf_op jit(solution)/shard_map/all_to_all | solution.py:105
  332.2 6.9 copy-start.2
  437.5 257.2 %all-to-all-start.1 = ((bf16[2,1024,2048]{1,0,2:T(2,128)(2,1)}), bf16[2,1024,2048]{1,0,2:T(2,128)(2,1)}, u32[]{:S(2)}, u32[]{:S(2)}) async-start(bf16[2,1024,2048]{1,0,2:T(2,128)(2,1)} %pad_maximum_fusion), calls=%async_computation.1 | async-start | bytes 16777216 | tf_op jit(solution)/shard_map/all_to_all | solution.py:110
  752.2 14.9 %copy-start.4 = (bf16[1,1024,2048]{2,1,0:T(8,128)(2,1)S(1)}, bf16[1,1024,2048]{2,1,0:T(8,128)(2,1)}, u32[]{:S(2)}) copy-start(bf16[1,1024,2048]{2,1,0:T(8,128)(2,1)} %copy.159) | copy-start | bytes 12582916
  752.2 28.3 %slice-start.2 = ((s8[8388608]{0:T(1024)(128)(4,1)}), s8[4194304]{0:T(1024)(128)(4,1)S(1)}, s32[]{:S(2)}) async-start(s8[8388608]{0:T(1024)(128)(4,1)} %bitcast.114), calls=%async_computation.4 | async-start | bytes 8388608
  752.2 40.4 %slice-start = ((s8[8388608]{0:T(1024)(128)(4,1)}), s8[4194304]{0:T(1024)(128)(4,1)S(1)}, s32[]{:S(2)}) async-start(s8[8388608]{0:T(1024)(128)(4,1)} %bitcast.112), calls=%async_computation.2 | async-start | bytes 8388608
  767.1 13.4 %slice-start.3 = ((s8[8388608]{0:T(1024)(128)(4,1)}), s8[4194304]{0:T(1024)(128)(4,1)S(1)}, s32[]{:S(2)}) async-start(s8[8388608]{0:T(1024)(128)(4,1)} %bitcast.114), calls=%async_computation.5 | async-start | bytes 8388608
  767.1 25.5 %slice-start.1 = ((s8[8388608]{0:T(1024)(128)(4,1)}), s8[4194304]{0:T(1024)(128)(4,1)S(1)}, s32[]{:S(2)}) async-start(s8[8388608]{0:T(1024)(128)(4,1)} %bitcast.112), calls=%async_computation.3 | async-start | bytes 8388608
  780.5 12.2 %copy-start.3 = (bf16[1,1024,2048]{2,1,0:T(8,128)(2,1)S(1)}, bf16[1,1024,2048]{2,1,0:T(8,128)(2,1)}, u32[]{:S(2)}) copy-start(bf16[1,1024,2048]{2,1,0:T(8,128)(2,1)} %copy.158) | copy-start | bytes 12582916
  792.7 12.2 %copy-start.7 = (bf16[1024,2048]{1,0:T(8,128)(2,1)S(1)}, bf16[1024,2048]{1,0:T(8,128)(2,1)}, u32[]{:S(2)}) copy-start(bf16[1024,2048]{1,0:T(8,128)(2,1)} %add_convert_fusion.1) | copy-start | bytes 12582916
